TPU v7x, 32 devices: a whole 2x2x4 slice. The times are simulated.
32 devices in a mesh: tile: 2 (over y), strip: 4 (over x, core), focus: 4 (over z).
Axes of the slice: x: 2, y: 2, z: 4, core: 2. Of those that a mesh axis runs over, the one named last changes fastest.
Arguments:
- phi: float32 [512, 2048], P(('tile', 'strip')), parts along dimension 0, may hold values from -6 to 6
- target: int32 [512, 2048], P(('tile', 'strip')), parts along dimension 0, may hold values 0 or 1
- defocus_ids: int32 [8], P(('tile', 'focus')), parts along dimension 0, may hold values from 0 to 30
- kernels: float32 [2, 4, 48, 512], replicated, may hold values from -16 to 16
- psi: float32 [48, 512], replicated, may hold values from -3.140625 to 3.140625
- row_freqs: int32 [48], replicated, may hold values from -96 to 95, as said below
- col_freqs: int32 [512], replicated, may hold values from -1024 to 1023, as said below
Outputs:
- phi_next: float32 [512, 2048], P(('tile', 'strip')), parts along dimension 0
There are 2 independent parts, one for each index of `tile`. A program takes and returns all parts, laid end to end along the dimension named above; an argument that names none is the same for every part. Nothing has to cross between parts.
Inputs may be any that keep to these rules, and one draw needn't show every extreme that they name: `row_freqs`: distinct whole frequencies; the lowest and highest of the range are always among them. `col_freqs`: distinct whole frequencies; the lowest and highest of the range are always among them.
All inputs are finite; a program needn't handle non-finite values. No bound on the sum of `target` on one device may be relied on, other than what follows from the above.
Results may differ from a plain program's by a relative error of at most 0.02.
Values may be sent and summed in bfloat16 or wider, within the bound.
No kernel may reach another device: no remote copies, remote signals or barrier semaphores. Data moves between devices by JAX's collectives and lax.ppermute only.
A program may use at most 64 MiB of HBM per device.

v0:
```python
import jax
import jax.numpy as jnp
from jax import lax
from jax.sharding import PartitionSpec as P

MARGIN = 64
LEVELS = 31
SWEEPS = 2
slope_resist = 4.0
level_resist = 0.5
step_size = 1.0
flow_rate = 0.2


def padded_2(block, sides, width):
    for axis, dim in sides:
        count = lax.axis_size(axis)
        forward = [(i, i + 1) for i in range(count - 1)]
        backward = [(target, source) for source, target in forward]
        low = lax.ppermute(
            lax.slice_in_dim(block, block.shape[dim] - width, None, axis=dim), axis, forward
        )
        high = lax.ppermute(lax.slice_in_dim(block, 0, width, axis=dim), axis, backward)
        block = jnp.concatenate([low, block, high], axis=dim)
    return block


def tables(freq_list, period, length):
    positions = jnp.arange(length, dtype=jnp.int32)
    phase_int = jnp.mod(freq_list[:, None] * positions[None, :], period)
    angles = phase_int.astype(jnp.float32) * (2.0 * jnp.pi / period)
    return (jnp.cos(angles).astype(jnp.bfloat16), jnp.sin(angles).astype(jnp.bfloat16))


def product(lhs_mat, rhs_mat):
    return jnp.dot(lhs_mat, rhs_mat, preferred_element_type=jnp.float32)


def product_t(lhs_mat, rhs_mat):
    return lax.dot_general(
        lhs_mat, rhs_mat, (((1,), (1,)), ((), ())), preferred_element_type=jnp.float32
    )


def exact_t(lhs_mat, rhs_mat):
    return lax.dot_general(
        lhs_mat.astype(jnp.float32),
        rhs_mat,
        (((0,), (0,)), ((), ())),
        precision=lax.Precision.HIGHEST,
        preferred_element_type=jnp.float32,
    )


def spectral_rows(cos_part, sin_part, y_re, y_im):
    z_re = exact_t(cos_part, y_re) - exact_t(sin_part, y_im)
    z_im = exact_t(cos_part, y_im) + exact_t(sin_part, y_re)
    return jnp.concatenate([z_re, z_im], axis=1).astype(jnp.bfloat16)


def curvature_step(extended):
    padded = jnp.pad(extended, ((0, 0), (1, 1)))
    center = padded[1:-1, 1:-1]
    upper_row = padded[2:, 1:-1]
    lower_row = padded[:-2, 1:-1]
    right_col = padded[1:-1, 2:]
    left_col = padded[1:-1, :-2]
    diagonal = padded[2:, 2:] - padded[2:, :-2] - padded[:-2, 2:] + padded[:-2, :-2]
    grad_x = 0.5 * (upper_row - lower_row)
    grad_y = 0.5 * (right_col - left_col)
    second_x = upper_row - 2.0 * center + lower_row
    second_y = right_col - 2.0 * center + left_col
    cross_term = 0.25 * diagonal
    flow_term = (
        second_x * grad_y * grad_y - 2.0 * grad_x * grad_y * cross_term + second_y * grad_x * grad_x
    ) / (1.0 + grad_x * grad_x + grad_y * grad_y)
    return center + flow_rate * flow_term


def on_device(phi, target, defocus_ids, kernels, psi, row_freqs, col_freqs):
    strip_rows, col_count = phi.shape
    spectrum = psi.shape[1]
    kernel_count = kernels.shape[1]
    window_rows = strip_rows + 2 * MARGIN
    scale_norm = 1.0 / jnp.sqrt(jnp.float32(window_rows * col_count))
    row_cos, row_sin = tables(row_freqs, window_rows, window_rows)
    col_cos, col_sin = tables(col_freqs, col_count, col_count)
    forward = jnp.concatenate([col_cos, -col_sin], axis=0)
    adjoint = jnp.concatenate([col_sin, col_cos], axis=0)
    inner_cos = row_cos[:, MARGIN : MARGIN + strip_rows]
    inner_sin = row_sin[:, MARGIN : MARGIN + strip_rows]
    mask_bf = jnp.tanh(phi).astype(jnp.bfloat16)
    window = padded_2(mask_bf, (("strip", 0),), MARGIN)
    spec_pair = product_t(window, forward).astype(jnp.bfloat16)
    cos_half = product(row_cos, spec_pair)
    sin_half = product(row_sin, spec_pair)
    s_re = scale_norm * (cos_half[:, :spectrum] + sin_half[:, spectrum:])
    s_im = scale_norm * (cos_half[:, spectrum:] - sin_half[:, :spectrum])
    middle = (LEVELS - 1) / 2.0
    defocus = (defocus_ids[0].astype(jnp.float32) - middle) / middle
    phase_turn = defocus * psi
    cos_turn = jnp.cos(phase_turn)
    sin_turn = jnp.sin(phase_turn)
    k_re = kernels[0] * cos_turn - kernels[1] * sin_turn
    k_im = kernels[0] * sin_turn + kernels[1] * cos_turn
    g_pair = jnp.concatenate([k_re * s_re - k_im * s_im, k_re * s_im + k_im * s_re], axis=2).astype(
        jnp.bfloat16
    )
    head_part = jnp.einsum("fr,kfc->krc", inner_cos, g_pair, preferred_element_type=jnp.float32)
    tail_part = jnp.einsum("fr,kfc->krc", inner_sin, g_pair, preferred_element_type=jnp.float32)
    q_re = head_part[..., :spectrum] - tail_part[..., spectrum:]
    q_im = head_part[..., spectrum:] + tail_part[..., :spectrum]
    q_pair = (
        jnp.concatenate([q_re, q_im], axis=2)
        .astype(jnp.bfloat16)
        .reshape(kernel_count * strip_rows, 2 * spectrum)
    )
    e_re = (scale_norm * product(q_pair, forward)).reshape(kernel_count, strip_rows, col_count)
    e_im = (scale_norm * product(q_pair, adjoint)).reshape(kernel_count, strip_rows, col_count)
    intensity = jnp.mean(e_re * e_re + e_im * e_im, axis=0)
    resist = jax.nn.sigmoid(slope_resist * (intensity - level_resist))
    weight = (
        4.0
        * slope_resist
        / kernel_count
        * (resist - target.astype(jnp.float32))
        * resist
        * (1.0 - resist)
    )
    v_re = (weight * e_re).astype(jnp.bfloat16).reshape(kernel_count * strip_rows, col_count)
    v_im = (weight * e_im).astype(jnp.bfloat16).reshape(kernel_count * strip_rows, col_count)
    u_pair = (
        (product_t(v_re, forward) + product_t(v_im, adjoint))
        .astype(jnp.bfloat16)
        .reshape(kernel_count, strip_rows, 2 * spectrum)
    )
    head_back = jnp.einsum("fr,krc->kfc", inner_cos, u_pair, preferred_element_type=jnp.float32)
    tail_back = jnp.einsum("fr,krc->kfc", inner_sin, u_pair, preferred_element_type=jnp.float32)
    w_re = scale_norm * (head_back[..., :spectrum] + tail_back[..., spectrum:])
    w_im = scale_norm * (head_back[..., spectrum:] - tail_back[..., :spectrum])
    y_re = jnp.sum(k_re * w_re + k_im * w_im, axis=0)
    y_im = jnp.sum(k_re * w_im - k_im * w_re, axis=0)
    y_re, y_im = (
        lax.psum(y_re.astype(jnp.bfloat16), "focus").astype(jnp.float32),
        lax.psum(y_im.astype(jnp.bfloat16), "focus").astype(jnp.float32),
    )
    stacked = jnp.stack([y_re, y_im])[None]
    beside_all = padded_2(stacked.astype(jnp.bfloat16), (("strip", 0),), 1).astype(stacked.dtype)
    own_rows = spectral_rows(inner_cos, inner_sin, y_re, y_im)
    prev_rows = spectral_rows(
        row_cos[:, MARGIN + strip_rows :],
        row_sin[:, MARGIN + strip_rows :],
        beside_all[0, 0],
        beside_all[0, 1],
    )
    next_rows = spectral_rows(
        row_cos[:, :MARGIN], row_sin[:, :MARGIN], beside_all[2, 0], beside_all[2, 1]
    )
    grad_rows = scale_norm * product(
        jnp.concatenate([own_rows, prev_rows, next_rows], axis=0), forward
    )
    folded = grad_rows[:strip_rows]
    folded = (
        folded.at[:MARGIN]
        .add(grad_rows[strip_rows : strip_rows + MARGIN])
        .at[strip_rows - MARGIN :]
        .add(grad_rows[strip_rows + MARGIN :])
    )
    mask_slope = 1.0 - jnp.tanh(phi) * jnp.tanh(phi)
    level_set = phi - step_size * mask_slope * folded
    for counter in range(SWEEPS):
        extended_set = padded_2(level_set.astype(jnp.bfloat16), (("strip", 0),), 1).astype(
            level_set.dtype
        )
        level_set = curvature_step(extended_set)
    return level_set


def solution(mesh):
    return jax.shard_map(
        on_device,
        mesh=mesh,
        in_specs=(
            P(("tile", "strip"), None),
            P(("tile", "strip"), None),
            P(("tile", "focus")),
            P(),
            P(),
            P(),
            P(),
        ),
        out_specs=P(("tile", "strip"), None),
        check_vma=False,
    )
```

profile of v0, /device:TPU:1, one launch (start us, length us, event | category | flops | bytes accessed | tf_op | source)
XLA Modules:
  0.0 142.4 jit_solution(1823749973720386125)
XLA Ops:
  6.5 1.1 tanh_convert_fusion
  7.7 1.9 %collective-permute-start.1 = (bf16[64,2048]{1,0:T(8,128)(2,1)S(1)}, bf16[64,2048]{1,0:T(8,128)(2,1)S(1)}, u32[]{:S(2)}, u32[]{:S(2)}) collective-permute-start(bf16[64,2048]{1,0:T(8,128)(2,1)S(1)} %tanh_convert_fusion), channel_id=1, source_target_pairs={{4,0},{8,4},{12,8},{5,1},{9,5},{13,9},{6,2},{10,6},{14,10},{7,3},{... | collective-permute-start | bytes 786440 | tf_op jit(solution)/shard_map/ppermute | solution.py:23
  9.6 4.5 %collective-permute-start = (bf16[64,2048]{1,0:T(8,128)(2,1)S(1)}, bf16[64,2048]{1,0:T(8,128)(2,1)S(1)}, u32[]{:S(2)}, u32[]{:S(2)}) collective-permute-start(bf16[64,2048]{1,0:T(8,128)(2,1)S(1)} %tanh_convert_fusion), channel_id=1, source_target_pairs={{0,4},{4,8},{8,12},{1,5},{5,9},{9,13},{2,6},{6,10},{10,14},{3,7},{... | collective-permute-start | bytes 786440 | tf_op jit(solution)/shard_map/ppermute | solution.py:20
  14.1 18.9 %sine_convert_fusion = (bf16[512,2048]{1,0:T(8,128)(2,1)S(1)}, bf16[512,2048]{1,0:T(8,128)(2,1)S(1)}) fusion(s32[512]{0:T(512)} %param.21), kind=kLoop, calls=%fused_computation.8 | loop fusion | flops 16777216 | bytes 4196352 | tf_op jit(solution)/shard_map/convert_element_type | solution.py:32
  33.0 16.9 %fusion.22 = bf16[512,2048]{1,0:T(8,128)(2,1)S(1)} fusion(s32[512]{0:T(512)S(1)} %copy-done.9), kind=kLoop, calls=%fused_computation.50 | loop fusion | flops 18874368 | bytes 2099200 | tf_op jit(solution)/shard_map/neg | solution.py:88
  50.9 1.5 %convolution_convert_fusion = bf16[192,1024]{1,0:T(8,128)(2,1)S(1)} fusion(bf16[64,2048]{1,0:T(8,128)(2,1)S(1)} %collective-permute-done.1, bf16[64,2048]{1,0:T(8,128)(2,1)S(1)} %tanh_convert_fusion, bf16[64,2048]{1,0:T(8,128)(2,1)S(1)} %collective-permute-done, bf16[512,2048]{1,0:T(8,128)(2,1)S(1)} %fusion.22, bf16[512,2048]{1,0:T(8,128)(2,1)S(1)} %get-tuple-element.65), kind=kOutput, calls=%fused_computation.28 | convolution fusion | flops 816250880 | bytes 5373952 | tf_op jit(solution)/shard_map/dot_general | solution.py:40
  54.0 0.4 convolution_bitcast_fusion
  55.1 1.3 convolution_multiply_fusion.1
  56.4 3.0 %multiply_add_fusion = (f32[256,2048]{1,0:T(8,128)}, f32[256,2048]{1,0:T(8,128)}) fusion(f32[256,2048]{1,0:T(8,128)S(1)} %convolution_multiply_fusion.1, bf16[512,2048]{1,0:T(8,128)(2,1)S(1)} %get-tuple-element.65, bf16[512,2048]{1,0:T(8,128)(2,1)S(1)} %get-tuple-element.64, bf16[256,512]{1,0:T(8,128)(2,1)S(1)} %bitcast.84, bf16[256,512]{1,0:T(8,128)(2,1)S(1)} %bitcast.82), kind=kOutput, calls=%fused_computation.21 | convolution fusion | flops 1085276160 | bytes 11010048 | tf_op jit(solution)/shard_map/dot_general | solution.py:36
  59.4 1.8 %reduce_sum.27 = f32[64,2048]{1,0:T(8,128)S(1)} reduce(f32[4,64,2048]{2,1,0:T(8,128)} %bitcast.76, f32[]{:T(128)} %constant.126.clone.1), dimensions={0}, to_apply=%region_0.1 | reduce | flops 393216 | bytes 2621444 | tf_op jit(solution)/shard_map/reduce_sum | solution.py:120
  61.1 1.3 subtract_multiply_fusion
  62.4 2.9 %fusion.8 = (bf16[256,2048]{1,0:T(8,128)(2,1)S(1)}, bf16[256,2048]{1,0:T(8,128)(2,1)S(1)}) fusion(f32[256,2048]{1,0:T(8,128)} %get-tuple-element.69, f32[64,2048]{1,0:T(8,128)S(1)} %subtract_multiply_fusion, f32[256,2048]{1,0:T(8,128)} %copy-done), kind=kLoop, calls=%fused_computation.20 | loop fusion | flops 2097152 | bytes 6815744 | tf_op jit(solution)/shard_map/convert_element_type | solution.py:131
  65.4 1.3 fusion.107
  66.9 1.3 fusion.10
  68.8 0.9 add_reduce_fusion
  69.8 32.6 %all-reduce.5.cloned.1.call-done = (bf16[48,512]{1,0:T(8,128)(2,1)}, bf16[48,512]{1,0:T(8,128)(2,1)}) async-done(((bf16[48,512]{1,0:T(8,128)(2,1)}, bf16[48,512]{1,0:T(8,128)(2,1)}), (bf16[48,512]{1,0:T(8,128)(2,1)}, bf16[48,512]{1,0:T(8,128)(2,1)})) %all-reduce.5.cloned.1.call-update) | async-done | bytes 98320 | tf_op jit(solution)/shard_map/psum | solution.py:145
  102.4 1.0 pad_maximum_fusion.14
  103.4 4.7 %collective-permute-start.3 = (bf16[1,2,48,512]{3,2,1,0:T(8,128)(2,1)S(1)}, bf16[1,2,48,512]{3,2,1,0:T(8,128)(2,1)S(1)}, u32[]{:S(2)}, u32[]{:S(2)}) collective-permute-start(bf16[1,2,48,512]{3,2,1,0:T(8,128)(2,1)S(1)} %pad_maximum_fusion.14), channel_id=1, source_target_pairs={{4,0},{8,4},{12,8},{5,1},{9,5},{13,9},{6,2},{10,6},{14,10},{7,3},{... | collective-permute-start | bytes 294920 | tf_op jit(solution)/shard_map/ppermute | solution.py:23
  108.1 3.2 %collective-permute-start.2 = (bf16[1,2,48,512]{3,2,1,0:T(8,128)(2,1)S(1)}, bf16[1,2,48,512]{3,2,1,0:T(8,128)(2,1)S(1)}, u32[]{:S(2)}, u32[]{:S(2)}) collective-permute-start(bf16[1,2,48,512]{3,2,1,0:T(8,128)(2,1)S(1)} %pad_maximum_fusion.14), channel_id=1, source_target_pairs={{0,4},{4,8},{8,12},{1,5},{5,9},{9,13},{2,6},{6,10},{10,14},{3,7},{... | collective-permute-start | bytes 294920 | tf_op jit(solution)/shard_map/ppermute | solution.py:20
  111.2 1.0 fusion.89
  112.3 1.1 fusion.87
  113.3 1.1 fusion.12
  114.4 1.1 fusion.11
  117.0 1.0 convolution_multiply_fusion.2
  118.3 2.4 %collective-permute-start.4 = (bf16[1,2048]{1,0:T(2,128)(2,1)S(1)}, bf16[1,2048]{1,0:T(2,128)(2,1)S(1)}, u32[]{:S(2)}, u32[]{:S(2)}) collective-permute-start(bf16[1,2048]{1,0:T(2,128)(2,1)S(1)} %get-tuple-element.60), channel_id=1, source_target_pairs={{0,4},{4,8},{8,12},{1,5},{5,9},{9,13},{2,6},{6,10},{10,14},{3,7},{... | collective-permute-start | bytes 12296 | tf_op jit(solution)/shard_map/ppermute | solution.py:20
  120.7 1.9 %collective-permute-start.5 = (bf16[1,2048]{1,0:T(2,128)(2,1)S(1)}, bf16[1,2048]{1,0:T(2,128)(2,1)S(1)}, u32[]{:S(2)}, u32[]{:S(2)}) collective-permute-start(bf16[1,2048]{1,0:T(2,128)(2,1)S(1)} %get-tuple-element.61), channel_id=1, source_target_pairs={{4,0},{8,4},{12,8},{5,1},{9,5},{13,9},{6,2},{10,6},{14,10},{7,3},{... | collective-permute-start | bytes 12296 | tf_op jit(solution)/shard_map/ppermute | solution.py:23
  122.6 3.0 %collective-permute-done.5 = bf16[1,2048]{1,0:T(2,128)(2,1)S(1)} collective-permute-done((bf16[1,2048]{1,0:T(2,128)(2,1)S(1)}, bf16[1,2048]{1,0:T(2,128)(2,1)S(1)}, u32[]{:S(2)}, u32[]{:S(2)}) %collective-permute-start.5) | collective-permute-done | bytes 4128 | tf_op jit(solution)/shard_map/ppermute | solution.py:23
  125.8 1.0 add_convert_fusion
  126.8 1.9 %collective-permute-start.6 = (bf16[1,2048]{1,0:T(2,128)(2,1)S(1)}, bf16[1,2048]{1,0:T(2,128)(2,1)S(1)}, u32[]{:S(2)}, u32[]{:S(2)}) collective-permute-start(bf16[1,2048]{1,0:T(2,128)(2,1)S(1)} %get-tuple-element.58), channel_id=1, source_target_pairs={{0,4},{4,8},{8,12},{1,5},{5,9},{9,13},{2,6},{6,10},{10,14},{3,7},{... | collective-permute-start | bytes 12296 | tf_op jit(solution)/shard_map/ppermute | solution.py:20
  128.7 2.4 %collective-permute-start.7 = (bf16[1,2048]{1,0:T(2,128)(2,1)S(1)}, bf16[1,2048]{1,0:T(2,128)(2,1)S(1)}, u32[]{:S(2)}, u32[]{:S(2)}) collective-permute-start(bf16[1,2048]{1,0:T(2,128)(2,1)S(1)} %get-tuple-element.59), channel_id=1, source_target_pairs={{4,0},{8,4},{12,8},{5,1},{9,5},{13,9},{6,2},{10,6},{14,10},{7,3},{... | collective-permute-start | bytes 12296 | tf_op jit(solution)/shard_map/ppermute | solution.py:23
  131.1 2.6 %collective-permute-done.7 = bf16[1,2048]{1,0:T(2,128)(2,1)S(1)} collective-permute-done((bf16[1,2048]{1,0:T(2,128)(2,1)S(1)}, bf16[1,2048]{1,0:T(2,128)(2,1)S(1)}, u32[]{:S(2)}, u32[]{:S(2)}) %collective-permute-start.7) | collective-permute-done | bytes 4128 | tf_op jit(solution)/shard_map/ppermute | solution.py:23
  133.8 1.8 %multiply_add_fusion.1 = f32[64,2048]{1,0:T(8,128)} fusion(f32[66,2048]{1,0:T(8,128)S(1)} %maximum_convert_fusion.1), kind=kLoop, calls=%fused_computation.89 | loop fusion | flops 3670016 | bytes 2686976 | tf_op jit(solution)/shard_map/add | solution.py:77
  (53 shorter events, 5.2 us)
Async XLA Ops:
  6.5 95.9 %all-reduce.5.cloned.1.call-start = ((), (), s32[]{:S(2)}) async-start(), calls=%async_computation | async-start | bytes 196608 | tf_op jit(solution)/shard_map/psum | solution.py:145
  7.7 25.3 %copy-start.9 = (s32[512]{0:T(512)S(1)}, s32[512]{0:T(512)}, u32[]{:S(2)}) copy-start(s32[512]{0:T(512)} %param.21) | copy-start | bytes 6148
  7.7 43.2 %collective-permute-start.1 = (bf16[64,2048]{1,0:T(8,128)(2,1)S(1)}, bf16[64,2048]{1,0:T(8,128)(2,1)S(1)}, u32[]{:S(2)}, u32[]{:S(2)}) collective-permute-start(bf16[64,2048]{1,0:T(8,128)(2,1)S(1)} %tanh_convert_fusion), channel_id=1, source_target_pairs={{4,0},{8,4},{12,8},{5,1},{9,5},{13,9},{6,2},{10,6},{14,10},{7,3},{... | collective-permute-start | bytes 786440 | tf_op jit(solution)/shard_map/ppermute | solution.py:23
  9.6 41.3 %collective-permute-start = (bf16[64,2048]{1,0:T(8,128)(2,1)S(1)}, bf16[64,2048]{1,0:T(8,128)(2,1)S(1)}, u32[]{:S(2)}, u32[]{:S(2)}) collective-permute-start(bf16[64,2048]{1,0:T(8,128)(2,1)S(1)} %tanh_convert_fusion), channel_id=1, source_target_pairs={{0,4},{4,8},{8,12},{1,5},{5,9},{9,13},{2,6},{6,10},{10,14},{3,7},{... | collective-permute-start | bytes 786440 | tf_op jit(solution)/shard_map/ppermute | solution.py:20
  33.0 23.4 %copy-start.1 = (bf16[512,2048]{1,0:T(8,128)(2,1)}, bf16[512,2048]{1,0:T(8,128)(2,1)S(1)}, u32[]{:S(2)}) copy-start(bf16[512,2048]{1,0:T(8,128)(2,1)S(1)} %get-tuple-element.65) | copy-start | bytes 6291460
  33.0 23.4 %copy-start.4 = (bf16[512,2048]{1,0:T(8,128)(2,1)}, bf16[512,2048]{1,0:T(8,128)(2,1)S(1)}, u32[]{:S(2)}) copy-start(bf16[512,2048]{1,0:T(8,128)(2,1)S(1)} %get-tuple-element.64) | copy-start | bytes 6291460
  33.0 17.6 %copy-start.10 = (s32[48]{0:T(128)S(1)}, s32[48]{0:T(128)}, u32[]{:S(2)}) copy-start(s32[48]{0:T(128)} %param.20) | copy-start | bytes 580
  50.9 2.4 %copy-start.8 = (f32[48,512]{1,0:T(8,128)S(1)}, f32[48,512]{1,0:T(8,128)}, u32[]{:S(2)}) copy-start(f32[48,512]{1,0:T(8,128)} %param.19) | copy-start | bytes 294916
  52.5 1.2 copy-start.7
  56.4 3.0 %copy-start = (f32[256,2048]{1,0:T(8,128)}, f32[256,2048]{1,0:T(8,128)S(1)}, u32[]{:S(2)}) copy-start(f32[256,2048]{1,0:T(8,128)S(1)} %convolution_multiply_fusion.1) | copy-start | bytes 6291460
  62.4 2.9 %copy-start.2 = (bf16[512,2048]{1,0:T(8,128)(2,1)S(1)}, bf16[512,2048]{1,0:T(8,128)(2,1)}, u32[]{:S(2)}) copy-start(bf16[512,2048]{1,0:T(8,128)(2,1)} %copy-done.1) | copy-start | bytes 6291460
  65.4 1.6 %copy-start.5 = (bf16[512,2048]{1,0:T(8,128)(2,1)S(1)}, bf16[512,2048]{1,0:T(8,128)(2,1)}, u32[]{:S(2)}) copy-start(bf16[512,2048]{1,0:T(8,128)(2,1)} %copy-done.4) | copy-start | bytes 6291460
  102.4 14.6 %copy-start.3 = (bf16[512,2048]{1,0:T(8,128)(2,1)S(1)}, bf16[512,2048]{1,0:T(8,128)(2,1)}, u32[]{:S(2)}) copy-start(bf16[512,2048]{1,0:T(8,128)(2,1)} %copy-done.1) | copy-start | bytes 6291460
  103.4 12.5 %collective-permute-start.3 = (bf16[1,2,48,512]{3,2,1,0:T(8,128)(2,1)S(1)}, bf16[1,2,48,512]{3,2,1,0:T(8,128)(2,1)S(1)}, u32[]{:S(2)}, u32[]{:S(2)}) collective-permute-start(bf16[1,2,48,512]{3,2,1,0:T(8,128)(2,1)S(1)} %pad_maximum_fusion.14), channel_id=1, source_target_pairs={{4,0},{8,4},{12,8},{5,1},{9,5},{13,9},{6,2},{10,6},{14,10},{7,3},{... | collective-permute-start | bytes 294920 | tf_op jit(solution)/shard_map/ppermute | solution.py:23
  108.1 7.4 %collective-permute-start.2 = (bf16[1,2,48,512]{3,2,1,0:T(8,128)(2,1)S(1)}, bf16[1,2,48,512]{3,2,1,0:T(8,128)(2,1)S(1)}, u32[]{:S(2)}, u32[]{:S(2)}) collective-permute-start(bf16[1,2,48,512]{3,2,1,0:T(8,128)(2,1)S(1)} %pad_maximum_fusion.14), channel_id=1, source_target_pairs={{0,4},{4,8},{8,12},{1,5},{5,9},{9,13},{2,6},{6,10},{10,14},{3,7},{... | collective-permute-start | bytes 294920 | tf_op jit(solution)/shard_map/ppermute | solution.py:20
  117.0 1.1 copy-start.6
  118.3 4.3 %collective-permute-start.4 = (bf16[1,2048]{1,0:T(2,128)(2,1)S(1)}, bf16[1,2048]{1,0:T(2,128)(2,1)S(1)}, u32[]{:S(2)}, u32[]{:S(2)}) collective-permute-start(bf16[1,2048]{1,0:T(2,128)(2,1)S(1)} %get-tuple-element.60), channel_id=1, source_target_pairs={{0,4},{4,8},{8,12},{1,5},{5,9},{9,13},{2,6},{6,10},{10,14},{3,7},{... | collective-permute-start | bytes 12296 | tf_op jit(solution)/shard_map/ppermute | solution.py:20
  120.7 5.0 %collective-permute-start.5 = (bf16[1,2048]{1,0:T(2,128)(2,1)S(1)}, bf16[1,2048]{1,0:T(2,128)(2,1)S(1)}, u32[]{:S(2)}, u32[]{:S(2)}) collective-permute-start(bf16[1,2048]{1,0:T(2,128)(2,1)S(1)} %get-tuple-element.61), channel_id=1, source_target_pairs={{4,0},{8,4},{12,8},{5,1},{9,5},{13,9},{6,2},{10,6},{14,10},{7,3},{... | collective-permute-start | bytes 12296 | tf_op jit(solution)/shard_map/ppermute | solution.py:23
  126.8 4.3 %collective-permute-start.6 = (bf16[1,2048]{1,0:T(2,128)(2,1)S(1)}, bf16[1,2048]{1,0:T(2,128)(2,1)S(1)}, u32[]{:S(2)}, u32[]{:S(2)}) collective-permute-start(bf16[1,2048]{1,0:T(2,128)(2,1)S(1)} %get-tuple-element.58), channel_id=1, source_target_pairs={{0,4},{4,8},{8,12},{1,5},{5,9},{9,13},{2,6},{6,10},{10,14},{3,7},{... | collective-permute-start | bytes 12296 | tf_op jit(solution)/shard_map/ppermute | solution.py:20
  128.7 5.0 %collective-permute-start.7 = (bf16[1,2048]{1,0:T(2,128)(2,1)S(1)}, bf16[1,2048]{1,0:T(2,128)(2,1)S(1)}, u32[]{:S(2)}, u32[]{:S(2)}) collective-permute-start(bf16[1,2048]{1,0:T(2,128)(2,1)S(1)} %get-tuple-element.59), channel_id=1, source_target_pairs={{4,0},{8,4},{12,8},{5,1},{9,5},{13,9},{6,2},{10,6},{14,10},{7,3},{... | collective-permute-start | bytes 12296 | tf_op jit(solution)/shard_map/ppermute | solution.py:23
Sparse Core Ops, SparseCore 0:
  69.9 32.4 all-reduce.4
where the time goes:
time: 143 us; the launch traced here: 142 us
  other arithmetic  49 us (34%)
  waiting for transfers between devices  38.2 us (27%)
  starting transfers between devices  22.9 us (16%)
  matrix products  17.2 us (12%)
  between operations  14.6 us (10%)
    psum x1, waiting for transfers between devices, on_device(): lax.psum(y_im.astype(jnp.bfloat16), 'focus').astype(jnp.float32)  32.6 us
    convert_element_type x1, other arithmetic, tables(): jnp.sin(angles).astype(jnp.bfloat16)  18.9 us
    neg x1, other arithmetic, on_device(): forward = jnp.concatenate([col_cos, -col_sin], axis=0)  16.9 us
    ppermute x4, starting transfers between devices, padded_2(): lax.ppermute(lax.slice_in_dim(block, block.shape[dim] - width, None, axis...  12 us
    ppermute x4, starting transfers between devices, padded_2(): lax.ppermute(lax.slice_in_dim(block, 0, width, axis=dim), axis, backward)  10.9 us
    dot_general x5, matrix products, product(): return jnp.dot(lhs_mat, rhs_mat, preferred_element_type=jnp.float32)  6.07 us
    dot_general x12, matrix products, exact_t(): lax.dot_general(lhs_mat.astype(jnp.float32), rhs_mat, (((0,), (0,)), ((),...  5.65 us
    ppermute x4, waiting for transfers between devices, padded_2(): lax.ppermute(lax.slice_in_dim(block, 0, width, axis=dim), axis, backward)  5.61 us
  transfers between devices with their start and end apart: 9, of which 3 were waited for; matrix products, arithmetic and copies ran while one was open for 29% of the time, Pallas kernels for 0%

commit v1 on v0

--- a/solution.py
+++ b/solution.py
@@ -142,7 +142,7 @@
     y_im = jnp.sum(k_re * w_im - k_im * w_re, axis=0)
     y_re, y_im = (
         lax.psum(y_re.astype(jnp.bfloat16), "focus").astype(jnp.float32),
-        lax.psum(y_im.astype(jnp.bfloat16), "focus").astype(jnp.float32),
+        jnp.sum(lax.all_gather(y_im.astype(jnp.bfloat16), "focus"), axis=0).astype(jnp.float32),
     )
     stacked = jnp.stack([y_re, y_im])[None]
     beside_all = padded_2(stacked.astype(jnp.bfloat16), (("strip", 0),), 1).astype(stacked.dtype)

time: 143 us -> 125 us (0.87)
  waiting for transfers between devices: 38.2 us -> 6.45 us
  blocking collectives: 0 us -> 27.4 us
  between operations: 14.6 us -> 1.22 us
  starting transfers between devices: 22.9 us -> 27.9 us
  matrix products: 17.2 us -> 14.1 us
  other arithmetic: 49 us -> 47.5 us
    psum x1 -> x0, waiting for transfers between devices: 32.6 us -> none  [on_device(): lax.psum(y_im.astype(jnp.bfloat16), 'focus').astype(jnp.float32)]
    psum x0 -> x1, blocking collectives: none -> 16.2 us  [on_device(): lax.psum(y_re.astype(jnp.bfloat16), 'focus').astype(jnp.float32)]
    all_gather x0 -> x1, blocking collectives: none -> 11.2 us  [on_device(): lax.all_gather(y_im.astype(jnp.bfloat16), 'focus')]
    dot_general x12, matrix products: 5.65 us -> 2.45 us  [exact_t(): lax.dot_general(lhs_mat.astype(jnp.float32), rhs_mat, (((0,), (0,)), ((),...]
    ppermute x4, starting transfers between devices: 10.9 us -> 14 us  [padded_2(): lax.ppermute(lax.slice_in_dim(block, 0, width, axis=dim), axis, backward)]
    ppermute x4, starting transfers between devices: 12 us -> 13.9 us  [padded_2(): lax.ppermute(lax.slice_in_dim(block, block.shape[dim] - width, None, axis...]
  transfers between devices with their start and end apart: 9 -> 8, of which waited for: 3 -> 3; matrix products, arithmetic and copies ran while one was open for 29% -> 30% of each run, Pallas kernels for 0% -> 0%
where the time goes in v1:
time: 125 us
  other arithmetic  47.5 us (38%)
  starting transfers between devices  27.9 us (22%)
  blocking collectives  27.4 us (22%)
  matrix products  14.1 us (11%)
  waiting for transfers between devices  6.45 us (5%)
    convert_element_type x1, other arithmetic, tables(): jnp.sin(angles).astype(jnp.bfloat16)  18.9 us
    neg x1, other arithmetic, on_device(): forward = jnp.concatenate([col_cos, -col_sin], axis=0)  16.9 us
    psum x1, blocking collectives, on_device(): lax.psum(y_re.astype(jnp.bfloat16), 'focus').astype(jnp.float32)  16.2 us
    ppermute x4, starting transfers between devices, padded_2(): lax.ppermute(lax.slice_in_dim(block, 0, width, axis=dim), axis, backward)  14 us
    ppermute x4, starting transfers between devices, padded_2(): lax.ppermute(lax.slice_in_dim(block, block.shape[dim] - width, None, axis...  13.9 us
    all_gather x1, blocking collectives, on_device(): lax.all_gather(y_im.astype(jnp.bfloat16), 'focus')  11.2 us
    dot_general x5, matrix products, product(): return jnp.dot(lhs_mat, rhs_mat, preferred_element_type=jnp.float32)  6.08 us
    ppermute x4, waiting for transfers between devices, padded_2(): lax.ppermute(lax.slice_in_dim(block, 0, width, axis=dim), axis, backward)  5.61 us
  transfers between devices with their start and end apart: 8, of which 3 were waited for; matrix products, arithmetic and copies ran while one was open for 30% of the time, Pallas kernels for 0%

profile of v1, /device:TPU:1, one launch (start us, length us, event | category | flops | bytes accessed | tf_op | source)
XLA Modules:
  0.0 124.9 jit_solution(2084387285716563858)
XLA Ops:
  0.0 1.1 tanh_convert_fusion
  1.1 1.9 %collective-permute-start.1 = (bf16[64,2048]{1,0:T(8,128)(2,1)S(1)}, bf16[64,2048]{1,0:T(8,128)(2,1)S(1)}, u32[]{:S(2)}, u32[]{:S(2)}) collective-permute-start(bf16[64,2048]{1,0:T(8,128)(2,1)S(1)} %tanh_convert_fusion), channel_id=1, source_target_pairs={{4,0},{8,4},{12,8},{5,1},{9,5},{13,9},{6,2},{10,6},{14,10},{7,3},{... | collective-permute-start | bytes 786440 | tf_op jit(solution)/shard_map/ppermute | solution.py:23
  3.1 4.5 %collective-permute-start = (bf16[64,2048]{1,0:T(8,128)(2,1)S(1)}, bf16[64,2048]{1,0:T(8,128)(2,1)S(1)}, u32[]{:S(2)}, u32[]{:S(2)}) collective-permute-start(bf16[64,2048]{1,0:T(8,128)(2,1)S(1)} %tanh_convert_fusion), channel_id=1, source_target_pairs={{0,4},{4,8},{8,12},{1,5},{5,9},{9,13},{2,6},{6,10},{10,14},{3,7},{... | collective-permute-start | bytes 786440 | tf_op jit(solution)/shard_map/ppermute | solution.py:20
  7.6 18.9 %sine_convert_fusion = (bf16[512,2048]{1,0:T(8,128)(2,1)S(1)}, bf16[512,2048]{1,0:T(8,128)(2,1)S(1)}) fusion(s32[512]{0:T(512)} %param.21), kind=kLoop, calls=%fused_computation.8 | loop fusion | flops 16777216 | bytes 4196352 | tf_op jit(solution)/shard_map/convert_element_type | solution.py:32
  26.5 16.9 %fusion.22 = bf16[512,2048]{1,0:T(8,128)(2,1)S(1)} fusion(s32[512]{0:T(512)S(1)} %copy-done.9), kind=kLoop, calls=%fused_computation.50 | loop fusion | flops 18874368 | bytes 2099200 | tf_op jit(solution)/shard_map/neg | solution.py:88
  44.4 1.6 %convolution_convert_fusion = bf16[192,1024]{1,0:T(8,128)(2,1)S(1)} fusion(bf16[64,2048]{1,0:T(8,128)(2,1)S(1)} %collective-permute-done.1, bf16[64,2048]{1,0:T(8,128)(2,1)S(1)} %tanh_convert_fusion, bf16[64,2048]{1,0:T(8,128)(2,1)S(1)} %collective-permute-done, bf16[512,2048]{1,0:T(8,128)(2,1)S(1)} %fusion.22, bf16[512,2048]{1,0:T(8,128)(2,1)S(1)} %get-tuple-element.63), kind=kOutput, calls=%fused_computation.28 | convolution fusion | flops 816250880 | bytes 5373952 | tf_op jit(solution)/shard_map/dot_general | solution.py:40
  46.0 0.4 fusion.93
  46.4 0.4 fusion.92
  46.8 0.4 fusion.60
  47.5 0.4 convolution_bitcast_fusion
  47.9 0.4 convolution_bitcast_fusion.1
  48.6 1.3 %convolution_multiply_fusion.1 = f32[256,2048]{1,0:T(8,128)S(1)} fusion(bf16[256,512]{1,0:T(8,128)(2,1)S(1)} %bitcast.85, bf16[256,512]{1,0:T(8,128)(2,1)S(1)} %bitcast.83, bf16[512,2048]{1,0:T(8,128)(2,1)S(1)} %fusion.22, bf16[512,2048]{1,0:T(8,128)(2,1)S(1)} %get-tuple-element.63), kind=kOutput, calls=%fused_computation.16 | convolution fusion | flops 1083703296 | bytes 6815744 | tf_op jit(solution)/shard_map/dot_general | solution.py:36
  49.9 3.0 %multiply_add_fusion = (f32[256,2048]{1,0:T(8,128)}, f32[256,2048]{1,0:T(8,128)}) fusion(f32[256,2048]{1,0:T(8,128)S(1)} %convolution_multiply_fusion.1, bf16[512,2048]{1,0:T(8,128)(2,1)S(1)} %get-tuple-element.63, bf16[512,2048]{1,0:T(8,128)(2,1)S(1)} %get-tuple-element.62, bf16[256,512]{1,0:T(8,128)(2,1)S(1)} %bitcast.86, bf16[256,512]{1,0:T(8,128)(2,1)S(1)} %bitcast.84), kind=kOutput, calls=%fused_computation.21 | convolution fusion | flops 1085276160 | bytes 11010048 | tf_op jit(solution)/shard_map/dot_general | solution.py:36
  52.8 1.8 %reduce_sum.39 = f32[64,2048]{1,0:T(8,128)S(1)} reduce(f32[4,64,2048]{2,1,0:T(8,128)} %bitcast.77, f32[]{:T(128)} %constant.127.clone.1), dimensions={0}, to_apply=%region_0.1 | reduce | flops 393216 | bytes 2621444 | tf_op jit(solution)/shard_map/reduce_sum | solution.py:120
  54.6 1.3 %subtract_multiply_fusion = f32[64,2048]{1,0:T(8,128)S(1)} fusion(s32[64,2048]{1,0:T(8,128)} %param.16, f32[64,2048]{1,0:T(8,128)S(1)} %reduce_sum.39), kind=kLoop, calls=%fused_computation.91 | loop fusion | flops 1572864 | bytes 1572864 | tf_op jit(solution)/shard_map/mul | solution.py:123
  55.9 2.9 %fusion.8 = (bf16[256,2048]{1,0:T(8,128)(2,1)S(1)}, bf16[256,2048]{1,0:T(8,128)(2,1)S(1)}) fusion(f32[256,2048]{1,0:T(8,128)} %get-tuple-element.67, f32[64,2048]{1,0:T(8,128)S(1)} %subtract_multiply_fusion, f32[256,2048]{1,0:T(8,128)} %copy-done), kind=kLoop, calls=%fused_computation.20 | loop fusion | flops 2097152 | bytes 6815744 | tf_op jit(solution)/shard_map/convert_element_type | solution.py:131
  58.8 1.3 %fusion.107 = f32[256,1024]{1,0:T(8,128)S(1)} fusion(bf16[256,2048]{1,0:T(8,128)(2,1)S(1)} %get-tuple-element.53, bf16[512,2048]{1,0:T(8,128)(2,1)S(1)} %fusion.22, bf16[512,2048]{1,0:T(8,128)(2,1)S(1)} %copy-done.2), kind=kOutput, calls=%fused_computation.182 | convolution fusion | flops 1082130432 | bytes 6291456 | tf_op jit(solution)/shard_map/dot_general | solution.py:40
  60.4 1.3 %fusion.10 = bf16[256,1024]{1,0:T(8,128)(2,1)S(1)} fusion(f32[256,1024]{1,0:T(8,128)S(1)} %fusion.107, bf16[256,2048]{1,0:T(8,128)(2,1)S(1)} %get-tuple-element.52, bf16[512,2048]{1,0:T(8,128)(2,1)S(1)} %copy-done.2, bf16[512,2048]{1,0:T(8,128)(2,1)S(1)} %copy-done.5), kind=kOutput, calls=%fused_computation.25 | convolution fusion | flops 1082654720 | bytes 6815744 | tf_op jit(solution)/shard_map/dot_general | solution.py:40
  62.6 16.2 %psum.7 = bf16[48,512]{1,0:T(8,128)(2,1)S(1)} all-reduce(bf16[48,512]{1,0:T(8,128)(2,1)S(1)} %get-tuple-element.45), channel_id=1, replica_groups=mesh['tile'=2,'strip'=4,'focus'=4] {'focus'}, use_global_device_ids=true, to_apply=%region_2.3 | all-reduce | flops 24576 | bytes 98304 | tf_op jit(solution)/shard_map/psum | solution.py:144
  79.1 11.2 %all-gather = bf16[192,512]{1,0:T(8,128)(2,1)S(1)} all-gather(bf16[48,512]{1,0:T(8,128)(2,1)S(1)} %get-tuple-element.46), channel_id=2, replica_groups=mesh['tile'=2,'strip'=4,'focus'=4] {'focus'}, dimensions={0}, use_global_device_ids=true | all-gather | bytes 245760 | tf_op jit(solution)/shard_map/all_gather | solution.py:145
  90.3 7.8 %collective-permute-start.3 = (bf16[1,2,48,512]{3,2,1,0:T(8,128)(2,1)S(1)}, bf16[1,2,48,512]{3,2,1,0:T(8,128)(2,1)S(1)}, u32[]{:S(2)}, u32[]{:S(2)}) collective-permute-start(bf16[1,2,48,512]{3,2,1,0:T(8,128)(2,1)S(1)} %pad_maximum_fusion.14), channel_id=1, source_target_pairs={{4,0},{8,4},{12,8},{5,1},{9,5},{13,9},{6,2},{10,6},{14,10},{7,3},{... | collective-permute-start | bytes 294920 | tf_op jit(solution)/shard_map/ppermute | solution.py:23
  98.1 3.1 %collective-permute-start.2 = (bf16[1,2,48,512]{3,2,1,0:T(8,128)(2,1)S(1)}, bf16[1,2,48,512]{3,2,1,0:T(8,128)(2,1)S(1)}, u32[]{:S(2)}, u32[]{:S(2)}) collective-permute-start(bf16[1,2,48,512]{3,2,1,0:T(8,128)(2,1)S(1)} %pad_maximum_fusion.14), channel_id=1, source_target_pairs={{0,4},{4,8},{8,12},{1,5},{5,9},{9,13},{2,6},{6,10},{10,14},{3,7},{... | collective-permute-start | bytes 294920 | tf_op jit(solution)/shard_map/ppermute | solution.py:20
  102.0 0.8 collective-permute-done.2
  104.4 1.0 convolution_multiply_fusion.2
  105.7 4.3 %collective-permute-start.4 = (bf16[1,2048]{1,0:T(2,128)(2,1)S(1)}, bf16[1,2048]{1,0:T(2,128)(2,1)S(1)}, u32[]{:S(2)}, u32[]{:S(2)}) collective-permute-start(bf16[1,2048]{1,0:T(2,128)(2,1)S(1)} %get-tuple-element.58), channel_id=1, source_target_pairs={{0,4},{4,8},{8,12},{1,5},{5,9},{9,13},{2,6},{6,10},{10,14},{3,7},{... | collective-permute-start | bytes 12296 | tf_op jit(solution)/shard_map/ppermute | solution.py:20
  110.0 1.9 %collective-permute-start.5 = (bf16[1,2048]{1,0:T(2,128)(2,1)S(1)}, bf16[1,2048]{1,0:T(2,128)(2,1)S(1)}, u32[]{:S(2)}, u32[]{:S(2)}) collective-permute-start(bf16[1,2048]{1,0:T(2,128)(2,1)S(1)} %get-tuple-element.59), channel_id=1, source_target_pairs={{4,0},{8,4},{12,8},{5,1},{9,5},{13,9},{6,2},{10,6},{14,10},{7,3},{... | collective-permute-start | bytes 12296 | tf_op jit(solution)/shard_map/ppermute | solution.py:23
  112.0 3.0 %collective-permute-done.5 = bf16[1,2048]{1,0:T(2,128)(2,1)S(1)} collective-permute-done((bf16[1,2048]{1,0:T(2,128)(2,1)S(1)}, bf16[1,2048]{1,0:T(2,128)(2,1)S(1)}, u32[]{:S(2)}, u32[]{:S(2)}) %collective-permute-start.5) | collective-permute-done | bytes 4128 | tf_op jit(solution)/shard_map/ppermute | solution.py:23
  115.1 1.0 add_convert_fusion
  116.1 1.9 %collective-permute-start.6 = (bf16[1,2048]{1,0:T(2,128)(2,1)S(1)}, bf16[1,2048]{1,0:T(2,128)(2,1)S(1)}, u32[]{:S(2)}, u32[]{:S(2)}) collective-permute-start(bf16[1,2048]{1,0:T(2,128)(2,1)S(1)} %get-tuple-element.56), channel_id=1, source_target_pairs={{0,4},{4,8},{8,12},{1,5},{5,9},{9,13},{2,6},{6,10},{10,14},{3,7},{... | collective-permute-start | bytes 12296 | tf_op jit(solution)/shard_map/ppermute | solution.py:20
  118.0 2.4 %collective-permute-start.7 = (bf16[1,2048]{1,0:T(2,128)(2,1)S(1)}, bf16[1,2048]{1,0:T(2,128)(2,1)S(1)}, u32[]{:S(2)}, u32[]{:S(2)}) collective-permute-start(bf16[1,2048]{1,0:T(2,128)(2,1)S(1)} %get-tuple-element.57), channel_id=1, source_target_pairs={{4,0},{8,4},{12,8},{5,1},{9,5},{13,9},{6,2},{10,6},{14,10},{7,3},{... | collective-permute-start | bytes 12296 | tf_op jit(solution)/shard_map/ppermute | solution.py:23
  120.4 2.6 %collective-permute-done.7 = bf16[1,2048]{1,0:T(2,128)(2,1)S(1)} collective-permute-done((bf16[1,2048]{1,0:T(2,128)(2,1)S(1)}, bf16[1,2048]{1,0:T(2,128)(2,1)S(1)}, u32[]{:S(2)}, u32[]{:S(2)}) %collective-permute-start.7) | collective-permute-done | bytes 4128 | tf_op jit(solution)/shard_map/ppermute | solution.py:23
  123.1 1.8 %multiply_add_fusion.1 = f32[64,2048]{1,0:T(8,128)} fusion(f32[66,2048]{1,0:T(8,128)S(1)} %maximum_convert_fusion.1), kind=kLoop, calls=%fused_computation.89 | loop fusion | flops 3670016 | bytes 2686976 | tf_op jit(solution)/shard_map/add | solution.py:77
  (53 shorter events, 5.0 us)
Async XLA Ops:
  1.1 25.3 %copy-start.9 = (s32[512]{0:T(512)S(1)}, s32[512]{0:T(512)}, u32[]{:S(2)}) copy-start(s32[512]{0:T(512)} %param.21) | copy-start | bytes 6148
  1.1 43.2 %collective-permute-start.1 = (bf16[64,2048]{1,0:T(8,128)(2,1)S(1)}, bf16[64,2048]{1,0:T(8,128)(2,1)S(1)}, u32[]{:S(2)}, u32[]{:S(2)}) collective-permute-start(bf16[64,2048]{1,0:T(8,128)(2,1)S(1)} %tanh_convert_fusion), channel_id=1, source_target_pairs={{4,0},{8,4},{12,8},{5,1},{9,5},{13,9},{6,2},{10,6},{14,10},{7,3},{... | collective-permute-start | bytes 786440 | tf_op jit(solution)/shard_map/ppermute | solution.py:23
  3.1 41.3 %collective-permute-start = (bf16[64,2048]{1,0:T(8,128)(2,1)S(1)}, bf16[64,2048]{1,0:T(8,128)(2,1)S(1)}, u32[]{:S(2)}, u32[]{:S(2)}) collective-permute-start(bf16[64,2048]{1,0:T(8,128)(2,1)S(1)} %tanh_convert_fusion), channel_id=1, source_target_pairs={{0,4},{4,8},{8,12},{1,5},{5,9},{9,13},{2,6},{6,10},{10,14},{3,7},{... | collective-permute-start | bytes 786440 | tf_op jit(solution)/shard_map/ppermute | solution.py:20
  26.4 23.4 %copy-start.1 = (bf16[512,2048]{1,0:T(8,128)(2,1)}, bf16[512,2048]{1,0:T(8,128)(2,1)S(1)}, u32[]{:S(2)}) copy-start(bf16[512,2048]{1,0:T(8,128)(2,1)S(1)} %get-tuple-element.63) | copy-start | bytes 6291460
  26.4 23.4 %copy-start.4 = (bf16[512,2048]{1,0:T(8,128)(2,1)}, bf16[512,2048]{1,0:T(8,128)(2,1)S(1)}, u32[]{:S(2)}) copy-start(bf16[512,2048]{1,0:T(8,128)(2,1)S(1)} %get-tuple-element.62) | copy-start | bytes 6291460
  26.5 17.6 %copy-start.10 = (s32[48]{0:T(128)S(1)}, s32[48]{0:T(128)}, u32[]{:S(2)}) copy-start(s32[48]{0:T(128)} %param.20) | copy-start | bytes 580
  44.4 2.4 %copy-start.8 = (f32[48,512]{1,0:T(8,128)S(1)}, f32[48,512]{1,0:T(8,128)}, u32[]{:S(2)}) copy-start(f32[48,512]{1,0:T(8,128)} %param.19) | copy-start | bytes 294916
  45.9 1.2 copy-start.7
  49.8 3.0 %copy-start = (f32[256,2048]{1,0:T(8,128)}, f32[256,2048]{1,0:T(8,128)S(1)}, u32[]{:S(2)}) copy-start(f32[256,2048]{1,0:T(8,128)S(1)} %convolution_multiply_fusion.1) | copy-start | bytes 6291460
  55.9 2.9 %copy-start.2 = (bf16[512,2048]{1,0:T(8,128)(2,1)S(1)}, bf16[512,2048]{1,0:T(8,128)(2,1)}, u32[]{:S(2)}) copy-start(bf16[512,2048]{1,0:T(8,128)(2,1)} %copy-done.1) | copy-start | bytes 6291460
  58.8 1.6 %copy-start.5 = (bf16[512,2048]{1,0:T(8,128)(2,1)S(1)}, bf16[512,2048]{1,0:T(8,128)(2,1)}, u32[]{:S(2)}) copy-start(bf16[512,2048]{1,0:T(8,128)(2,1)} %copy-done.4) | copy-start | bytes 6291460
  90.3 14.1 %copy-start.3 = (bf16[512,2048]{1,0:T(8,128)(2,1)S(1)}, bf16[512,2048]{1,0:T(8,128)(2,1)}, u32[]{:S(2)}) copy-start(bf16[512,2048]{1,0:T(8,128)(2,1)} %copy-done.1) | copy-start | bytes 6291460
  90.3 12.9 %collective-permute-start.3 = (bf16[1,2,48,512]{3,2,1,0:T(8,128)(2,1)S(1)}, bf16[1,2,48,512]{3,2,1,0:T(8,128)(2,1)S(1)}, u32[]{:S(2)}, u32[]{:S(2)}) collective-permute-start(bf16[1,2,48,512]{3,2,1,0:T(8,128)(2,1)S(1)} %pad_maximum_fusion.14), channel_id=1, source_target_pairs={{4,0},{8,4},{12,8},{5,1},{9,5},{13,9},{6,2},{10,6},{14,10},{7,3},{... | collective-permute-start | bytes 294920 | tf_op jit(solution)/shard_map/ppermute | solution.py:23
  98.1 4.7 %collective-permute-start.2 = (bf16[1,2,48,512]{3,2,1,0:T(8,128)(2,1)S(1)}, bf16[1,2,48,512]{3,2,1,0:T(8,128)(2,1)S(1)}, u32[]{:S(2)}, u32[]{:S(2)}) collective-permute-start(bf16[1,2,48,512]{3,2,1,0:T(8,128)(2,1)S(1)} %pad_maximum_fusion.14), channel_id=1, source_target_pairs={{0,4},{4,8},{8,12},{1,5},{5,9},{9,13},{2,6},{6,10},{10,14},{3,7},{... | collective-permute-start | bytes 294920 | tf_op jit(solution)/shard_map/ppermute | solution.py:20
  104.4 1.1 copy-start.6
  105.7 6.2 %collective-permute-start.4 = (bf16[1,2048]{1,0:T(2,128)(2,1)S(1)}, bf16[1,2048]{1,0:T(2,128)(2,1)S(1)}, u32[]{:S(2)}, u32[]{:S(2)}) collective-permute-start(bf16[1,2048]{1,0:T(2,128)(2,1)S(1)} %get-tuple-element.58), channel_id=1, source_target_pairs={{0,4},{4,8},{8,12},{1,5},{5,9},{9,13},{2,6},{6,10},{10,14},{3,7},{... | collective-permute-start | bytes 12296 | tf_op jit(solution)/shard_map/ppermute | solution.py:20
  110.0 5.0 %collective-permute-start.5 = (bf16[1,2048]{1,0:T(2,128)(2,1)S(1)}, bf16[1,2048]{1,0:T(2,128)(2,1)S(1)}, u32[]{:S(2)}, u32[]{:S(2)}) collective-permute-start(bf16[1,2048]{1,0:T(2,128)(2,1)S(1)} %get-tuple-element.59), channel_id=1, source_target_pairs={{4,0},{8,4},{12,8},{5,1},{9,5},{13,9},{6,2},{10,6},{14,10},{7,3},{... | collective-permute-start | bytes 12296 | tf_op jit(solution)/shard_map/ppermute | solution.py:23
  116.1 4.3 %collective-permute-start.6 = (bf16[1,2048]{1,0:T(2,128)(2,1)S(1)}, bf16[1,2048]{1,0:T(2,128)(2,1)S(1)}, u32[]{:S(2)}, u32[]{:S(2)}) collective-permute-start(bf16[1,2048]{1,0:T(2,128)(2,1)S(1)} %get-tuple-element.56), channel_id=1, source_target_pairs={{0,4},{4,8},{8,12},{1,5},{5,9},{9,13},{2,6},{6,10},{10,14},{3,7},{... | collective-permute-start | bytes 12296 | tf_op jit(solution)/shard_map/ppermute | solution.py:20
  118.0 5.0 %collective-permute-start.7 = (bf16[1,2048]{1,0:T(2,128)(2,1)S(1)}, bf16[1,2048]{1,0:T(2,128)(2,1)S(1)}, u32[]{:S(2)}, u32[]{:S(2)}) collective-permute-start(bf16[1,2048]{1,0:T(2,128)(2,1)S(1)} %get-tuple-element.57), channel_id=1, source_target_pairs={{4,0},{8,4},{12,8},{5,1},{9,5},{13,9},{6,2},{10,6},{14,10},{7,3},{... | collective-permute-start | bytes 12296 | tf_op jit(solution)/shard_map/ppermute | solution.py:23
